TPU v7x, 32 devices: a whole 2x2x4 slice. The times are simulated.
32 devices in a mesh: groups: 2 (over y), blk: 4 (over z), side: 2 (over x), tp: 2 (over core).
Axes of the slice: x: 2, y: 2, z: 4, core: 2. Of those that a mesh axis runs over, the one named last changes fastest.
Arguments:
- queries: bfloat16 [4, 512, 4096], P(('groups', 'side'), 'blk', 'tp'), parts along dimension 0, may hold values from -8 to 8
- key_rows: bfloat16 [4, 512, 256], P(('groups', 'side'), 'blk', 'tp'), parts along dimension 0, may hold values from -8 to 8
- value_rows: bfloat16 [4, 512, 256], P(('groups', 'side'), 'blk', 'tp'), parts along dimension 0, may hold values from -6 to 6
- segments: int32 [4, 512], P(('groups', 'side'), 'blk'), parts along dimension 0, may hold values from 0 to 1, never falling along the last dimension, each value on 1 to 384 neighbouring positions
- hidden_entry_rows: bfloat16 [4, 512, 4096], P(('groups', 'side'), 'blk', 'tp'), parts along dimension 0, may hold values from -6 to 6
- expert_ids: int32 [4, 512, 8], P(('groups', 'side'), 'blk'), parts along dimension 0, may hold values from 0 to 127, all different within a row; in each aligned block of 128 rows (0 to 127, 128 to 255, ..., all dimensions but the last counted through in order) at most 10 rows name the same one
- route_weight: float32 [4, 512, 8], P(('groups', 'side'), 'blk'), parts along dimension 0, may hold values from 0.2 to 1
- w_gate: bfloat16 [4, 2048, 1536], P('blk', 'tp', 'side'), may hold values from -0.09375 to 0.09375
- w_up: bfloat16 [4, 2048, 1536], P('blk', 'tp', 'side'), may hold values from -0.09375 to 0.09375
- w_down: bfloat16 [4, 1536, 2048], P('blk', 'side', 'tp'), may hold values from -0.15625 to 0.15625
Outputs:
- attended: bfloat16 [4, 512, 4096], P(('groups', 'side'), 'blk', 'tp'), parts along dimension 0
- moe_out: bfloat16 [4, 512, 4096], P(('groups', 'side'), 'blk', 'tp'), parts along dimension 0
There are 2 independent parts, one for each index of `groups`. A program takes and returns all parts, laid end to end along the dimension named above; an argument that names none is the same for every part. Nothing has to cross between parts.
Inputs may be any that keep to these rules, and one draw needn't show every extreme that they name: `expert_ids`: in the 128 rows of one device (aligned blocks of rows of a sequence) no expert is named by more than 10 rows, and in some such block one is named by exactly 10; a row names 8 different experts. `segments`: document numbers never fall along a sequence; a document spans at most 384 positions, and one spans exactly that many.
All inputs are finite; a program needn't handle non-finite values.
Results may differ from a plain program's by a relative error of at most 0.02.
Values may be sent and summed in bfloat16 or wider, within the bound.
A program may use at most 64 MiB of HBM per device.

v0:
```python
import math

import jax
import jax.numpy as jnp
from jax import lax
from jax.sharding import PartitionSpec as P

HEAD_DIM = 128
CAP = 10


def passed_along(value, axis, steps):
    count = lax.axis_size(axis)
    pairs = [(source, (source + steps) % count) for source in range(count)]
    return lax.ppermute(value, axis, pairs)


def slot_choice(id_rows, experts, capacity):
    named = id_rows[:, :, None] == jnp.arange(experts, dtype=jnp.int32)[None, None, :]
    hits = jnp.sum(named.astype(jnp.int32), axis=1)
    ranks = jnp.cumsum(hits, axis=0) - hits
    levels = jnp.arange(capacity, dtype=jnp.int32)[None, :, None]
    return (hits.T[:, None, :] > 0) & (ranks.T[:, None, :] == levels)


def routing_slot_index(id_rows, experts, capacity):
    chosen = slot_choice(id_rows, experts, capacity)
    row_iota = jnp.arange(id_rows.shape[0], dtype=jnp.int32)
    index = jnp.sum(jnp.where(chosen, row_iota[None, None, :], 0), axis=2)
    valid = jnp.any(chosen, axis=2)
    return (index, valid)


def pick_rows(rows, index, valid):
    taken = jnp.take(rows, index, axis=0)
    return jnp.where(valid[..., None], taken, jnp.zeros((), rows.dtype))


def slot_weights(id_rows, weight_rows, experts, capacity):
    named = id_rows[:, :, None] == jnp.arange(experts, dtype=jnp.int32)[None, None, :]
    shares = jnp.sum(jnp.where(named, weight_rows[:, :, None], 0.0), axis=1)
    chosen = slot_choice(id_rows, experts, capacity)
    return chosen.astype(jnp.float32) * shares.T[:, None, :]


def body(
    queries,
    key_rows,
    value_rows,
    segments,
    hidden_entry_rows,
    expert_ids,
    route_weight,
    w_gate,
    w_up,
    w_down,
):
    length = queries.shape[1]
    head_size = HEAD_DIM
    kv_here = key_rows.shape[2] // head_size
    group = queries.shape[2] // (head_size * kv_here)
    query_portion = queries[0].reshape(length, kv_here, group, head_size)
    local_segment_labels = segments[0]
    query_pos = lax.axis_index("blk") * length + jnp.arange(length, dtype=jnp.int32)
    factor = 1.0 / math.sqrt(head_size)
    start_state = (
        jnp.full((length, kv_here, group), -1e30, jnp.float32),
        jnp.zeros((length, kv_here, group), jnp.float32),
        jnp.zeros((length, kv_here, group, head_size), jnp.float32),
    )
    key_piece = lax.all_gather(key_rows[0], "blk", axis=0, tiled=True)
    value_fragment = lax.all_gather(value_rows[0], "blk", axis=0, tiled=True)
    segment_piece = lax.all_gather(local_segment_labels, "blk", axis=0, tiled=True)
    rows_in = key_piece.shape[0]
    width = math.gcd(rows_in, 512)

    def one_block(block_index, state):
        row_max, totals, accumulated = state
        begin = block_index * width
        key_tile_block = lax.dynamic_slice_in_dim(key_piece, begin, width, 0).reshape(
            width, kv_here, head_size
        )
        value_block = lax.dynamic_slice_in_dim(value_fragment, begin, width, 0).reshape(
            width, kv_here, head_size
        )
        segment_block = lax.dynamic_slice_in_dim(segment_piece, begin, width, 0)
        key_pos = begin + jnp.arange(width, dtype=jnp.int32)
        allowed = (key_pos[None, :] <= query_pos[:, None]) & (
            segment_block[None, :] == local_segment_labels[:, None]
        )
        masking = allowed[:, None, None, :]
        scores = (
            jnp.einsum(
                "wsmz,usz->wsmu", query_portion, key_tile_block, preferred_element_type=jnp.float32
            )
            * factor
        )
        scores = jnp.where(masking, scores, -1e30)
        new_max = jnp.maximum(row_max, jnp.max(scores, axis=3))
        rescale = jnp.exp(row_max - new_max)
        weights = jnp.where(masking, jnp.exp(scores - new_max[..., None]), 0.0)
        totals = totals * rescale + jnp.sum(weights, axis=3)
        update = jnp.einsum(
            "jzre,ezm->jzrm",
            weights.astype(jnp.bfloat16),
            value_block,
            preferred_element_type=jnp.float32,
        )
        accumulated = accumulated * rescale[..., None] + update
        return (new_max, totals, accumulated)

    row_max, totals, accumulated = lax.fori_loop(0, rows_in // width, one_block, start_state)
    attended = (
        (accumulated / totals[..., None])
        .astype(jnp.bfloat16)
        .reshape(1, length, group * kv_here * head_size)
    )
    experts = lax.axis_size("blk") // 2
    capacity = CAP
    ff_here = w_gate.shape[2]
    quarter = hidden_entry_rows.shape[2] // 2
    index, valid = routing_slot_index(expert_ids[0], experts, capacity)
    taken = pick_rows(hidden_entry_rows[0], index, valid)
    outgoing = (
        taken.reshape(experts, capacity, 2, quarter)
        .transpose(2, 0, 1, 3)
        .reshape(2 * experts, capacity, quarter)[:, None]
    )
    arrived = lax.all_to_all(outgoing, "blk", split_axis=0, concat_axis=0, tiled=True)
    shards = lax.all_gather(arrived, "side", axis=1, tiled=True)
    gate_piece = jnp.einsum("bscd,df->bscf", shards, w_gate[0], preferred_element_type=jnp.float32)
    up_piece = jnp.einsum("bscd,df->bscf", shards, w_up[0], preferred_element_type=jnp.float32)
    projected = jnp.concatenate([gate_piece, up_piece], axis=3)
    gate_part = projected[..., :ff_here]
    up_part = projected[..., ff_here:]
    gate_sum, up_sum = (
        lax.psum(gate_part.astype(jnp.bfloat16), "tp").astype(jnp.float32),
        lax.psum(up_part.astype(jnp.bfloat16), "tp").astype(jnp.float32),
    )
    both_sums = jnp.stack([gate_sum, up_sum])
    partner_sums = passed_along(
        both_sums.astype(jnp.bfloat16), "blk", lax.axis_size("blk") // 2
    ).astype(both_sums.dtype)
    full_sums = both_sums + partner_sums
    hidden = (jax.nn.silu(full_sums[0]) * full_sums[1]).astype(jnp.bfloat16)
    part_out = jnp.einsum(
        "bscf,fd->bscd", hidden, w_down[0], preferred_element_type=jnp.float32
    ).astype(jnp.bfloat16)
    parts = lax.all_to_all(part_out, "side", split_axis=1, concat_axis=1, tiled=True)
    slot_out = jnp.sum(parts, axis=1, dtype=jnp.float32).astype(jnp.bfloat16)
    returned = lax.all_to_all(slot_out, "blk", split_axis=0, concat_axis=0, tiled=True)
    returned_split = returned.astype(jnp.float32).reshape(2, experts, capacity, quarter)
    own_weighted = slot_weights(expert_ids[0], route_weight[0], experts, capacity)
    mixed = jnp.einsum(
        "ecr,kecq->rkq", own_weighted, returned_split, precision=lax.Precision.HIGHEST
    )
    moe_out = mixed.reshape(mixed.shape[0], 2 * quarter).astype(jnp.bfloat16)[None]
    return (attended, moe_out)


def solution(mesh):
    placed = (
        P(("groups", "side"), "blk", "tp"),
        P(("groups", "side"), "blk", "tp"),
        P(("groups", "side"), "blk", "tp"),
        P(("groups", "side"), "blk"),
        P(("groups", "side"), "blk", "tp"),
        P(("groups", "side"), "blk", None),
        P(("groups", "side"), "blk", None),
        P("blk", "tp", "side"),
        P("blk", "tp", "side"),
        P("blk", "side", "tp"),
    )
    return jax.shard_map(
        body,
        mesh=mesh,
        in_specs=placed,
        out_specs=(P(("groups", "side"), "blk", "tp"), P(("groups", "side"), "blk", "tp")),
        check_vma=False,
    )
```

profile of v0, /device:TPU:0, one launch (start us, length us, event | category | flops | bytes accessed | tf_op | source)
XLA Modules:
  0.0 131.0 jit_solution(2119913399250369770)
XLA Ops:
  7.2 0.0 copy-start
  7.2 0.8 convert_reduce_fusion
  8.0 0.1 copy.47
  8.1 0.2 reduce_window_sum.12
  8.3 0.1 copy.49
  8.4 0.1 select_reduce_fusion
  8.5 0.1 fusion.50
  8.6 0.1 reshape.152
  8.7 1.8 %gather_fusion = bf16[20,2048]{1,0:T(8,128)(2,1)S(1)} fusion(bf16[128,2048]{1,0:T(8,128)(2,1)} %bitcast.124, s32[1024]{0:T(1024)S(1)} %pad_clamp_fusion), kind=kCustom, calls=%fused_computation | custom fusion | bytes 163920 | tf_op jit(solution)/shard_map/jit(_take)/gather | solution.py:35
  10.6 0.7 fusion.47
  11.3 6.3 %all-to-all-start = ((bf16[4,1,10,1024]{3,2,1,0:T(8,128)(2,1)}), bf16[4,1,10,1024]{3,2,1,0:T(8,128)(2,1)S(1)}, u32[]{:S(2)}, u32[]{:S(2)}) async-start(bf16[4,1,10,1024]{3,2,1,0:T(8,128)(2,1)} %bitcast.21), calls=%async_computation | async-start | bytes 262144 | tf_op jit(solution)/shard_map/all_to_all | solution.py:129
  17.7 0.0 all-reduce.3.cloned.1.call-start
  17.7 11.5 %all-gather = s32[1,512]{1,0:T(1,128)S(1)} all-gather(s32[1,128]{1,0:T(1,128)} %param.13), channel_id=2, replica_groups=mesh['groups'=2,'blk'=4,'side'=2,'tp'=2] {'blk'}, dimensions={1}, use_global_device_ids=true | all-gather | bytes 2560 | tf_op jit(solution)/shard_map/all_gather | solution.py:73
  29.2 0.8 fusion.41
  30.0 1.1 copy.62
  31.2 13.6 %all-gather.1 = bf16[1,512,128]{2,1,0:T(8,128)(2,1)S(1)} all-gather(bf16[1,128,128]{2,1,0:T(8,128)(2,1)} %param.11), channel_id=3, replica_groups=mesh['groups'=2,'blk'=4,'side'=2,'tp'=2] {'blk'}, dimensions={1}, use_global_device_ids=true | all-gather | bytes 163840 | tf_op jit(solution)/shard_map/all_gather | solution.py:71
  44.8 0.0 all-to-all-done
  44.8 5.6 %all_gather.15 = bf16[4,2,10,1024]{3,2,1,0:T(8,128)(2,1)S(1)} all-gather(bf16[4,1,10,1024]{3,2,1,0:T(8,128)(2,1)S(1)} %all-to-all-done), channel_id=1, replica_groups=mesh['groups'=2,'blk'=4,'side'=2,'tp'=2] {'side'}, dimensions={1}, use_global_device_ids=true | all-gather | bytes 245760 | tf_op jit(solution)/shard_map/all_gather | solution.py:130
  50.4 2.5 %fusion.33 = bf16[1,4,2,10,768]{4,3,2,1,0:T(8,128)(2,1)} fusion(bf16[4,2,10,1024]{3,2,1,0:T(8,128)(2,1)S(1)} %all_gather.15, bf16[1,1024,768]{2,1,0:T(8,128)(2,1)} %param.17), kind=kOutput, calls=%fused_computation.24 | convolution fusion | flops 125890560 | bytes 1859584 | tf_op jit(solution)/shard_map/bscd,df->bscf/dot_general | solution.py:131
  52.8 2.5 %fusion.30 = bf16[1,4,2,10,768]{4,3,2,1,0:T(8,128)(2,1)} fusion(bf16[4,2,10,1024]{3,2,1,0:T(8,128)(2,1)S(1)} %all_gather.15, bf16[1,1024,768]{2,1,0:T(8,128)(2,1)} %param.18), kind=kOutput, calls=%fused_computation.23 | convolution fusion | flops 125890560 | bytes 1859584 | tf_op jit(solution)/shard_map/bscd,df->bscf/dot_general | solution.py:132
  55.3 0.0 all-reduce.3.cloned.1.call-update
  55.3 2.7 %fusion = (f32[128,16]{0,1:T(8,128)S(1)}, f32[512,128,16]{1,0,2:T(8,128)}) fusion(pred[128,512]{0,1:T(8,128)(4,1)S(1)} %fusion.41, bf16[128,16,128]{2,1,0:T(8,128)(2,1)S(1)} %bitcast.123, bf16[1,512,128]{2,1,0:T(8,128)(2,1)S(1)} %all-gather.1), kind=kOutput, calls=%fused_computation.3 | convolution fusion | flops 271579136 | bytes 4923392 | tf_op jit(solution)/shard_map/while/body/eval_jaxpr/wsmz,usz->wsmu/dot_general | solution.py:93
  58.0 14.2 %all-reduce.3.cloned.1.call-done = (bf16[1,4,2,10,768]{4,3,2,1,0:T(8,128)(2,1)}, bf16[1,4,2,10,768]{4,3,2,1,0:T(8,128)(2,1)}) async-done(((bf16[1,4,2,10,768]{4,3,2,1,0:T(8,128)(2,1)}, bf16[1,4,2,10,768]{4,3,2,1,0:T(8,128)(2,1)}), (bf16[1,4,2,10,768]{4,3,2,1,0:T(8,128)(2,1)}, bf16[1,4,2,10,768]{4,3,2,1,0:T(8,128)(2,1)})) %all-reduce.3.cloned.1.call-update) | async-done | bytes 245776 | tf_op jit(solution)/shard_map/psum | solution.py:137
  72.2 0.9 constant_dynamic-update-slice_fusion.1
  73.2 0.9 constant_dynamic-update-slice_fusion
  74.1 2.8 %collective-permute-start = (bf16[2,4,2,10,768]{4,3,2,1,0:T(8,128)(2,1)S(1)}, bf16[2,4,2,10,768]{4,3,2,1,0:T(8,128)(2,1)S(1)}, u32[]{:S(2)}, u32[]{:S(2)}) collective-permute-start(bf16[2,4,2,10,768]{4,3,2,1,0:T(8,128)(2,1)S(1)} %constant_dynamic-update-slice_fusion), channel_id=1, source_target_pairs={{0,8},{4,12},{8,0},{12,4},{1,9},{5,13},{9,1},{13,5},{2,10},{6,14},... | collective-permute-start | bytes 737288 | tf_op jit(solution)/shard_map/ppermute | solution.py:15
  76.9 0.0 copy-start.1
  76.9 3.2 %fusion.1 = f32[128,16]{0,1:T(8,128)S(1)} fusion(f32[512,128,16]{1,0,2:T(8,128)} %get-tuple-element.48, f32[128,16]{0,1:T(8,128)S(1)} %broadcast_maximum_fusion, pred[128,512]{0,1:T(8,128)(4,1)S(1)} %fusion.41), kind=kLoop, calls=%fused_computation.4 | loop fusion | flops 5240832 | bytes 4276224 | tf_op jit(solution)/shard_map/while/body/eval_jaxpr/reduce_sum | solution.py:102
  80.1 14.7 %collective-permute-done = bf16[2,4,2,10,768]{4,3,2,1,0:T(8,128)(2,1)S(1)} collective-permute-done((bf16[2,4,2,10,768]{4,3,2,1,0:T(8,128)(2,1)S(1)}, bf16[2,4,2,10,768]{4,3,2,1,0:T(8,128)(2,1)S(1)}, u32[]{:S(2)}, u32[]{:S(2)}) %collective-permute-start) | collective-permute-done | bytes 245792 | tf_op jit(solution)/shard_map/ppermute | solution.py:15
  94.8 0.1 convert_add_fusion
  94.9 0.0 copy-done
  95.0 0.4 fusion.21
  95.4 0.8 copy.51
  96.2 3.4 %all-to-all-start.1 = ((bf16[4,2,10,1024]{3,0,2,1:T(4,128)(2,1)}), bf16[4,2,10,1024]{3,0,2,1:T(4,128)(2,1)S(1)}, u32[]{:S(2)}, u32[]{:S(2)}) async-start(bf16[4,2,10,1024]{3,0,2,1:T(4,128)(2,1)} %copy.51), calls=%async_computation.1 | async-start | bytes 327680 | tf_op jit(solution)/shard_map/all_to_all | solution.py:149
  99.6 0.0 copy-done.1
  99.6 0.1 copy.45
  99.8 12.3 %all-gather.2 = bf16[1,512,128]{1,2,0:T(8,128)(2,1)S(1)} all-gather(bf16[1,128,128]{1,2,0:T(8,128)(2,1)S(1)} %copy.45), channel_id=4, replica_groups=mesh['groups'=2,'blk'=4,'side'=2,'tp'=2] {'blk'}, dimensions={1}, use_global_device_ids=true | all-gather | bytes 163840 | tf_op jit(solution)/shard_map/all_gather | solution.py:72
  112.0 0.0 all-to-all-done.1
  112.0 0.1 reduce_sum.60
  112.1 0.7 copy.61
  112.8 3.9 %all-to-all-start.2 = ((bf16[4,10,1024]{2,1,0:T(8,128)(2,1)}), bf16[4,10,1024]{2,1,0:T(8,128)(2,1)S(1)}, u32[]{:S(2)}, u32[]{:S(2)}) async-start(bf16[4,10,1024]{2,1,0:T(8,128)(2,1)} %copy.61), calls=%async_computation.2 | async-start | bytes 262144 | tf_op jit(solution)/shard_map/all_to_all | solution.py:151
  116.7 0.0 copy-start.2
  116.7 0.0 copy-start.3
  116.7 3.4 %divide_convert_fusion = bf16[1,128,128,16]{2,1,3,0:T(8,128)(2,1)S(1)} fusion(f32[512,128,16]{1,0,2:T(8,128)} %get-tuple-element.48, f32[128,16]{0,1:T(8,128)S(1)} %broadcast_maximum_fusion, pred[128,512]{0,1:T(8,128)(4,1)S(1)} %fusion.41, f32[128,16]{0,1:T(8,128)S(1)} %get-tuple-element.46, f32[128,16]{0,1:T(8,128)S(1)} %get-tuple-element.45, ...), kind=kOutput, calls=%fused_computation.25 | convolution fusion | flops 274464768 | bytes 4939776 | tf_op jit(solution)/shard_map/while/body/eval_jaxpr/jzre,ezm->jzrm/dot_general | solution.py:103
  120.1 1.0 copy.55
  121.1 0.0 copy-done.2
  121.1 0.0 copy-done.3
  121.1 1.4 %all-to-all-done.2 = bf16[4,10,1024]{2,1,0:T(8,128)(2,1)S(1)} async-done(((bf16[4,10,1024]{2,1,0:T(8,128)(2,1)}), bf16[4,10,1024]{2,1,0:T(8,128)(2,1)S(1)}, u32[]{:S(2)}, u32[]{:S(2)}) %all-to-all-start.2) | async-done | bytes 81952 | tf_op jit(solution)/shard_map/all_to_all | solution.py:151
  122.6 0.1 copy.60
  122.7 1.4 %fusion.4 = bf16[1,128,2048]{2,1,0:T(8,128)(2,1)} fusion(bf16[2048,10,2]{0,2,1:T(2,128)(2,1)S(1)} %bitcast.125, f32[2,128]{1,0:T(2,128)S(1)} %bitcast.132, s32[2,128]{1,0:T(2,128)S(1)} %copy.49, pred[2,128]{1,0:T(4,128)(4,1)S(1)} %compare_bitcast_fusion), kind=kOutput, calls=%fused_computation.8 | convolution fusion | flops 63184384 | bytes 608512 | tf_op jit(solution)/shard_map/ecr,kecq->rkq/dot_general | solution.py:154
  (10 shorter events, 0.1 us)
Async XLA Ops:
  7.2 87.8 %copy-start = (bf16[1,768,1024]{2,1,0:T(8,128)(2,1)S(1)}, bf16[1,768,1024]{2,1,0:T(8,128)(2,1)}, u32[]{:S(2)}) copy-start(bf16[1,768,1024]{2,1,0:T(8,128)(2,1)} %param.19) | copy-start | bytes 4718596
  11.3 33.4 %all-to-all-start = ((bf16[4,1,10,1024]{3,2,1,0:T(8,128)(2,1)}), bf16[4,1,10,1024]{3,2,1,0:T(8,128)(2,1)S(1)}, u32[]{:S(2)}, u32[]{:S(2)}) async-start(bf16[4,1,10,1024]{3,2,1,0:T(8,128)(2,1)} %bitcast.21), calls=%async_computation | async-start | bytes 262144 | tf_op jit(solution)/shard_map/all_to_all | solution.py:129
  17.7 54.5 %all-reduce.3.cloned.1.call-start = ((), (), s32[]{:S(2)}) async-start(), calls=%async_computation.3 | async-start | bytes 786432 | tf_op jit(solution)/shard_map/psum | solution.py:137
  74.1 20.7 %collective-permute-start = (bf16[2,4,2,10,768]{4,3,2,1,0:T(8,128)(2,1)S(1)}, bf16[2,4,2,10,768]{4,3,2,1,0:T(8,128)(2,1)S(1)}, u32[]{:S(2)}, u32[]{:S(2)}) collective-permute-start(bf16[2,4,2,10,768]{4,3,2,1,0:T(8,128)(2,1)S(1)} %constant_dynamic-update-slice_fusion), channel_id=1, source_target_pairs={{0,8},{4,12},{8,0},{12,4},{1,9},{5,13},{9,1},{13,5},{2,10},{6,14},... | collective-permute-start | bytes 737288 | tf_op jit(solution)/shard_map/ppermute | solution.py:15
  76.9 22.8 %copy-start.1 = (bf16[1,128,128]{2,1,0:T(8,128)(2,1)S(1)}, bf16[1,128,128]{2,1,0:T(8,128)(2,1)}, u32[]{:S(2)}) copy-start(bf16[1,128,128]{2,1,0:T(8,128)(2,1)} %param.12) | copy-start | bytes 98308
  96.2 15.8 %all-to-all-start.1 = ((bf16[4,2,10,1024]{3,0,2,1:T(4,128)(2,1)}), bf16[4,2,10,1024]{3,0,2,1:T(4,128)(2,1)S(1)}, u32[]{:S(2)}, u32[]{:S(2)}) async-start(bf16[4,2,10,1024]{3,0,2,1:T(4,128)(2,1)} %copy.51), calls=%async_computation.1 | async-start | bytes 327680 | tf_op jit(solution)/shard_map/all_to_all | solution.py:149
  112.8 9.8 %all-to-all-start.2 = ((bf16[4,10,1024]{2,1,0:T(8,128)(2,1)}), bf16[4,10,1024]{2,1,0:T(8,128)(2,1)S(1)}, u32[]{:S(2)}, u32[]{:S(2)}) async-start(bf16[4,10,1024]{2,1,0:T(8,128)(2,1)} %copy.61), calls=%async_computation.2 | async-start | bytes 262144 | tf_op jit(solution)/shard_map/all_to_all | solution.py:151
  116.7 4.4 %copy-start.2 = (s32[1,128,8]{1,2,0:T(8,128)S(1)}, s32[1,128,8]{1,2,0:T(8,128)}, u32[]{:S(2)}) copy-start(s32[1,128,8]{1,2,0:T(8,128)} %param.15) | copy-start | bytes 12292
  116.7 4.5 %copy-start.3 = (f32[1,128,8]{1,2,0:T(8,128)S(1)}, f32[1,128,8]{1,2,0:T(8,128)}, u32[]{:S(2)}) copy-start(f32[1,128,8]{1,2,0:T(8,128)} %param.16) | copy-start | bytes 12292
Sparse Core Ops, SparseCore 0:
  55.4 16.7 all-reduce.2
where the time goes:
time: 132 us; the launch traced here: 131 us
  blocking collectives  43 us (33%)
  waiting for transfers between devices  30.4 us (23%)
  starting transfers between devices  16.4 us (12%)
  between operations  14.2 us (11%)
  matrix products  12.9 us (10%)
  local copies, waits for them, and re-layouts  7.85 us (6%)
  other arithmetic  6.27 us (5%)
    ppermute x1, waiting for transfers between devices, passed_along(): return lax.ppermute(value, axis, pairs)  14.7 us
    psum x1, waiting for transfers between devices, body(): lax.psum(gate_part.astype(jnp.bfloat16), 'tp').astype(jnp.float32)  14.2 us
    all_gather x1, blocking collectives, body(): key_piece = lax.all_gather(key_rows[0], 'blk', axis=0, tiled=True)  13.6 us
    all_gather x1, blocking collectives, body(): value_fragment = lax.all_gather(value_rows[0], 'blk', axis=0, tiled=True)  12.3 us
    all_gather x1, blocking collectives, body(): lax.all_gather(local_segment_labels, 'blk', axis=0, tiled=True)  11.5 us
    all_to_all x1, starting transfers between devices, body(): lax.all_to_all(outgoing, 'blk', split_axis=0, concat_axis=0, tiled=True)  6.35 us
    all_gather x1, blocking collectives, body(): shards = lax.all_gather(arrived, 'side', axis=1, tiled=True)  5.63 us
    unnamed x13, local copies, waits for them, and re-layouts  3.93 us
  transfers between devices with their start and end apart: 5, of which 3 were waited for; matrix products, arithmetic and copies ran while one was open for 9% of the time, Pallas kernels for 0%

commit v1 on v0

v1 whole, which is shorter than its diff:
```python
import functools
import math

import jax
import jax.numpy as jnp
from jax import lax
from jax.experimental import pallas as pl
from jax.experimental.pallas import tpu as pltpu
from jax.sharding import PartitionSpec as P

HEAD_DIM = 128
CAP = 10
PAD = 16
BF = jnp.bfloat16
F32 = jnp.float32
MESH = pl.DeviceIdType.MESH


def iota(shape, dim):
    return lax.broadcasted_iota(jnp.int32, shape, dim)


def dot(a, b):
    return jnp.dot(a, b, preferred_element_type=F32)


def kernel(
    nblk, nside,
    q_hbm, k_hbm, v_hbm, seg_ref, x_hbm, ids_ref, rw_ref, wg_hbm, wu_hbm, wd_hbm,
    att_hbm, moe_hbm,
    q_ref, kv, segs, x_ref, wg, wu, wd, att, moe,
    disp, xin, terms, terms_in, zs, zin, hid, po, pin, rs, rin,
    in_sem, out_sem,
    kv_ss, kv_rs, sg_ss, sg_rs, d_ss, d_rs, f_ss, f_rs, t_ss, t_rs, z_ss, z_rs,
    h_ss, h_rs, p_ss, p_rs, r_ss, r_rs,
):
    experts = nblk // 2
    b = lax.axis_index("blk")
    j = lax.axis_index("side")
    t = lax.axis_index("tp")
    length = q_ref.shape[0]
    heads = q_ref.shape[1] // HEAD_DIM
    quarter = x_ref.shape[1] // 2
    rp = po.shape[1]
    half = nside // 2

    def remote(src, dst, ss, rs_, **where):
        return pltpu.make_async_remote_copy(
            src_ref=src, dst_ref=dst, send_sem=ss, recv_sem=rs_,
            device_id=where, device_id_type=MESH,
        )

    def at_blk(d):
        return lax.rem(b + d, nblk)

    def at_side(d):
        return lax.rem(j + d, nside)

    loads = [
        pltpu.make_async_copy(x_hbm, x_ref, in_sem.at[0]),
        pltpu.make_async_copy(k_hbm, kv.at[b, 0], in_sem.at[1]),
        pltpu.make_async_copy(v_hbm, kv.at[b, 1], in_sem.at[2]),
        pltpu.make_async_copy(wg_hbm, wg, in_sem.at[3]),
        pltpu.make_async_copy(wu_hbm, wu, in_sem.at[4]),
        pltpu.make_async_copy(q_hbm, q_ref, in_sem.at[5]),
        pltpu.make_async_copy(wd_hbm, wd, in_sem.at[6]),
    ]
    for load in loads:
        load.start()

    barrier = pltpu.get_barrier_semaphore()
    for d in range(1, nblk):
        pl.semaphore_signal(barrier, inc=1, device_id={"blk": at_blk(d)}, device_id_type=MESH)
    for d in range(1, nside):
        pl.semaphore_signal(barrier, inc=1, device_id={"side": at_side(d)}, device_id_type=MESH)
    pl.semaphore_signal(barrier, inc=1, device_id={"tp": 1 - t}, device_id_type=MESH)

    ids = ids_ref[...]
    rw = rw_ref[...]
    ep = -(-experts // 8) * 8
    expert_of = iota((ep, length), 0)
    hits = jnp.zeros((ep, length), F32)
    shares = jnp.zeros((ep, length), F32)
    for p in range(ids.shape[0]):
        named = ids[p : p + 1, :] == expert_of
        hits = hits + jnp.where(named, 1.0, 0.0)
        shares = shares + jnp.where(named, rw[p : p + 1, :], 0.0)
    before = jnp.where(iota((length, length), 0) < iota((length, length), 1), 1.0, 0.0)
    ranks = dot(hits.astype(BF), before.astype(BF))
    level = iota((PAD, length), 0).astype(F32)
    picks, pulls = [], []
    for e in range(experts):
        chosen = (hits[e : e + 1, :] > 0.0) & (ranks[e : e + 1, :] == level)
        picks.append(jnp.where(chosen, 1.0, 0.0))
        pulls.append(jnp.where(chosen, shares[e : e + 1, :], 0.0))
    pick = jnp.concatenate(picks, axis=0)
    pull = jnp.concatenate(pulls, axis=0)
    segs[b] = seg_ref[...]
    loads[0].wait()
    taken = dot(pick.astype(BF), x_ref[...]).astype(BF)
    for s in range(nblk):
        e, k = s % experts, s // experts
        disp[s] = taken[e * PAD : (e + 1) * PAD, k * quarter : (k + 1) * quarter]
    xin[j, b] = disp[b]

    loads[1].wait()
    loads[2].wait()
    pl.semaphore_wait(barrier, nblk - 1 + nside - 1 + 1)

    sends = []
    for d in range(1, nblk):
        to = at_blk(d)
        copy = remote(disp.at[to], xin.at[j, b], d_ss.at[d], d_rs.at[b], blk=to)
        copy.start()
        sends.append(copy)
    for d in range(1, nside):
        to = at_side(d)
        copy = remote(xin.at[j, b], xin.at[j, b], f_ss.at[d, 0], f_rs.at[j, b], side=to)
        copy.start()
        sends.append(copy)

    def kv_copy(d):
        to = jnp.minimum(b + d, nblk - 1)
        return (
            remote(kv.at[b], kv.at[b], kv_ss.at[d], kv_rs.at[b], blk=to),
            remote(segs.at[b], segs.at[b], sg_ss.at[d], sg_rs.at[b], blk=to),
        )

    for d in range(1, nblk):
        @pl.when(b + d < nblk)
        def _():
            for copy in kv_copy(d):
                copy.start()

    for d in range(1, nblk):
        @pl.when(b + d < nblk)
        def _():
            kv[b + d] = jnp.zeros(kv.shape[1:], kv.dtype)
            segs[b + d] = jnp.zeros(segs.shape[1:], segs.dtype)

    order = []
    for step in range(1, nblk // 2 + 1):
        for d in (step, nblk - step):
            if d not in order:
                order.append(d)
    for d in order:
        source = at_blk(d)
        remote(disp.at[0], xin.at[j, source], d_ss.at[0], d_rs.at[source], blk=source).wait_recv()
        for d2 in range(1, nside):
            to = at_side(d2)
            copy = remote(
                xin.at[j, source], xin.at[j, source], f_ss.at[d2, d], f_rs.at[j, source], side=to
            )
            copy.start()
            sends.append(copy)

    m = iota((rp, nblk * PAD), 1)
    low = m & (PAD - 1)
    packed = (low < CAP) & ((m >> 4) * CAP + low == iota((rp, nblk * PAD), 0))
    pack = jnp.where(packed, 1.0, 0.0).astype(BF)
    r = iota((nblk * PAD, rp), 0)
    low = r & (PAD - 1)
    spread = (low < CAP) & ((r >> 4) * CAP + low == iota((nblk * PAD, rp), 1))
    unpack = jnp.where(spread, 1.0, 0.0).astype(BF)

    for d2 in range(1, nside):
        other = at_side(d2)
        for d in range(nblk):
            source = at_blk(d)
            remote(
                xin.at[other, source], xin.at[other, source], f_ss.at[0, 0],
                f_rs.at[other, source], side=other,
            ).wait_recv()
    rows = jnp.concatenate(
        [
            dot(pack, xin[s].reshape(nblk * PAD, quarter)).astype(BF)
            for s in range(nside)
        ],
        axis=0,
    )
    loads[3].wait()
    gate = dot(rows, wg[...]).astype(BF)
    for s in range(nside):
        terms[s, 0] = gate[s * rp : (s + 1) * rp]
    loads[4].wait()
    up = dot(rows, wu[...]).astype(BF)
    for s in range(nside):
        terms[s, 1] = up[s * rp : (s + 1) * rp]

    mine = pl.ds(t * half, half)
    theirs = pl.ds((1 - t) * half, half)
    copy = remote(terms.at[theirs], terms_in, t_ss, t_rs, tp=1 - t)
    copy.start()
    copy.wait()
    zs[...] = (terms[mine].astype(F32) + terms_in[...].astype(F32)).astype(BF)
    z_copy = remote(zs, zin, z_ss, z_rs, blk=at_blk(experts))
    z_copy.start()

    for d in range(1, nblk):
        @pl.when(b - d >= 0)
        def _():
            source = jnp.maximum(b - d, 0)
            remote(kv.at[source], kv.at[source], kv_ss.at[0], kv_rs.at[source], blk=source).wait_recv()
            remote(segs.at[source], segs.at[source], sg_ss.at[0], sg_rs.at[source], blk=source).wait_recv()
    loads[5].wait()
    keys_all = nblk * length
    seg_keys = jnp.concatenate([segs[s] for s in range(nblk)], axis=1)
    seg_own = jnp.broadcast_to(segs[b].astype(F32), (length, length)).T
    seg_col = seg_own[:, :1].astype(jnp.int32)
    allowed = (iota((length, keys_all), 1) <= b * length + iota((length, keys_all), 0)) & (
        seg_keys == seg_col
    )
    factor = 1.0 / math.sqrt(HEAD_DIM)
    key_all = kv[:, 0].reshape(keys_all, HEAD_DIM)
    value_all = kv[:, 1].reshape(keys_all, HEAD_DIM)
    unroll = 4 if nblk <= 8 else 1

    def some_heads(step, carry):
        for u in range(unroll):
            cols = pl.ds(pl.multiple_of((step * unroll + u) * HEAD_DIM, HEAD_DIM), HEAD_DIM)
            scores = lax.dot_general(
                q_ref[:, cols], key_all, (((1,), (1,)), ((), ())), preferred_element_type=F32
            )
            scores = jnp.where(allowed, scores * factor, -1e30)
            largest = jnp.max(scores, axis=1, keepdims=True)
            weights = jnp.exp(scores - largest)
            totals = jnp.sum(weights, axis=1, keepdims=True)
            att[:, cols] = (dot(weights.astype(BF), value_all) / totals).astype(BF)
        return carry

    lax.fori_loop(0, heads // unroll, some_heads, 0)
    att_out = pltpu.make_async_copy(att, att_hbm, out_sem.at[0])
    att_out.start()

    z_copy.wait()
    gate_sum = zs[:, 0].astype(F32) + zin[:, 0].astype(F32)
    up_sum = zs[:, 1].astype(F32) + zin[:, 1].astype(F32)
    hid[mine] = (jax.nn.silu(gate_sum) * up_sum).astype(BF)
    copy = remote(hid.at[mine], hid.at[mine], h_ss, h_rs, tp=1 - t)
    copy.start()
    loads[6].wait()
    copy.wait_send()
    remote(hid.at[theirs], hid.at[theirs], h_ss, h_rs, tp=1 - t).wait_recv()

    for d in range(1, nside):
        to = at_side(d)
        po[to] = dot(hid[to], wd[...]).astype(BF)
        copy = remote(po.at[to], pin.at[j], p_ss.at[d], p_rs.at[j], side=to)
        copy.start()
        sends.append(copy)
    total = dot(hid[j], wd[...]).astype(BF).astype(F32)
    for d in range(1, nside):
        source = at_side(d)
        remote(po.at[0], pin.at[source], p_ss.at[0], p_rs.at[source], side=source).wait_recv()
        total = total + pin[source].astype(F32)
    rs[...] = dot(unpack, total.astype(BF)).astype(BF).reshape(rs.shape)
    for d in range(1, nblk):
        to = at_blk(d)
        copy = remote(rs.at[to], rin.at[b], r_ss.at[d], r_rs.at[b], blk=to)
        copy.start()
        sends.append(copy)
    rin[b] = rs[b]

    width = -(-experts * PAD // 128) * 128
    if width > experts * PAD:
        pull = jnp.concatenate([pull, jnp.zeros((width - experts * PAD, length), F32)], axis=0)
    pull = pull.T[:, : experts * PAD]
    pull_a = pull.astype(BF)
    rest = pull - pull_a.astype(F32)
    pull_b = rest.astype(BF)
    pull_c = (rest - pull_b.astype(F32)).astype(BF)

    for d in order:
        source = at_blk(d)
        remote(rs.at[0], rin.at[source], r_ss.at[0], r_rs.at[source], blk=source).wait_recv()
    for k in range(2):
        back = rin[k * experts : (k + 1) * experts].reshape(experts * PAD, quarter)
        mixed = dot(pull_a, back) + dot(pull_b, back) + dot(pull_c, back)
        moe[:, k * quarter : (k + 1) * quarter] = mixed.astype(BF)
    moe_out = pltpu.make_async_copy(moe, moe_hbm, out_sem.at[1])
    moe_out.start()

    for copy in sends:
        copy.wait_send()
    for d in range(1, nblk):
        @pl.when(b + d < nblk)
        def _():
            for copy in kv_copy(d):
                copy.wait_send()
    att_out.wait()
    moe_out.wait()


def body(
    nblk, nside,
    queries, key_rows, value_rows, segments, hidden_entry_rows, expert_ids, route_weight,
    w_gate, w_up, w_down,
):
    length, width = queries.shape[1:]
    quarter, ff = w_gate.shape[1:]
    rp = -(-nblk * CAP // PAD) * PAD
    half = nside // 2
    vmem = pl.BlockSpec(memory_space=pltpu.VMEM)
    hbm = pl.BlockSpec(memory_space=pl.ANY)
    dma = pltpu.SemaphoreType.DMA
    attended, moe_out = pl.pallas_call(
        functools.partial(kernel, nblk, nside),
        out_shape=(
            jax.ShapeDtypeStruct((length, width), BF),
            jax.ShapeDtypeStruct((length, 2 * quarter), BF),
        ),
        in_specs=[hbm, hbm, hbm, vmem, hbm, vmem, vmem, hbm, hbm, hbm],
        out_specs=(hbm, hbm),
        scratch_shapes=[
            pltpu.VMEM((length, width), BF),
            pltpu.VMEM((nblk, 2, length, HEAD_DIM), BF),
            pltpu.VMEM((nblk, 1, length), jnp.int32),
            pltpu.VMEM((length, 2 * quarter), BF),
            pltpu.VMEM((quarter, ff), BF),
            pltpu.VMEM((quarter, ff), BF),
            pltpu.VMEM((ff, quarter), BF),
            pltpu.VMEM((length, width), BF),
            pltpu.VMEM((length, 2 * quarter), BF),
            pltpu.VMEM((nblk, PAD, quarter), BF),
            pltpu.VMEM((nside, nblk, PAD, quarter), BF),
            pltpu.VMEM((nside, 2, rp, ff), BF),
            pltpu.VMEM((half, 2, rp, ff), BF),
            pltpu.VMEM((half, 2, rp, ff), BF),
            pltpu.VMEM((half, 2, rp, ff), BF),
            pltpu.VMEM((nside, rp, ff), BF),
            pltpu.VMEM((nside, rp, quarter), BF),
            pltpu.VMEM((nside, rp, quarter), BF),
            pltpu.VMEM((nblk, PAD, quarter), BF),
            pltpu.VMEM((nblk, PAD, quarter), BF),
            dma((7,)),
            dma((2,)),
            dma((nblk,)), dma((nblk,)),
            dma((nblk,)), dma((nblk,)),
            dma((nblk,)), dma((nblk,)),
            dma((nside, nblk)), dma((nside, nblk)),
            dma, dma, dma, dma, dma, dma,
            dma((nside,)), dma((nside,)),
            dma((nblk,)), dma((nblk,)),
        ],
        compiler_params=pltpu.CompilerParams(
            collective_id=0, has_side_effects=True, vmem_limit_bytes=56 * 1024 * 1024
        ),
    )(
        queries[0], key_rows[0], value_rows[0], segments, hidden_entry_rows[0],
        jnp.swapaxes(expert_ids[0], 0, 1), jnp.swapaxes(route_weight[0], 0, 1),
        w_gate[0], w_up[0], w_down[0],
    )
    return attended[None], moe_out[None]


def solution(mesh):
    rows = P(("groups", "side"), "blk", "tp")
    placed = (
        rows, rows, rows,
        P(("groups", "side"), "blk"),
        rows,
        P(("groups", "side"), "blk", None),
        P(("groups", "side"), "blk", None),
        P("blk", "tp", "side"),
        P("blk", "tp", "side"),
        P("blk", "side", "tp"),
    )
    return jax.shard_map(
        functools.partial(body, mesh.shape["blk"], mesh.shape["side"]),
        mesh=mesh,
        in_specs=placed,
        out_specs=(rows, rows),
        check_vma=False,
    )
```

time: 132 us -> 40.4 us (0.31)
  blocking collectives: 43 us -> 0 us
  Pallas kernels: 0 us -> 35.8 us
  waiting for transfers between devices: 30.4 us -> 0 us
  starting transfers between devices: 16.4 us -> 0 us
  between operations: 14.2 us -> 0.64 us
  matrix products: 12.9 us -> 0 us
  other arithmetic: 6.27 us -> 0 us
  local copies, waits for them, and re-layouts: 7.85 us -> 3.76 us
    all_gather x4 -> x0, blocking collectives: 43 us -> none  [the longest x1 13.6 us: body(): key_piece = lax.all_gather(key_rows[0], 'blk', axis=0, tiled=True)]
    pallas_call x0 -> x1, Pallas kernels: none -> 35.8 us  [body(): pl.pallas_call(functools.partial(kernel, nblk, nside), out_shape=(jax.Sha...]
    ppermute x1 -> x0, waiting for transfers between devices: 14.7 us -> none  [passed_along(): return lax.ppermute(value, axis, pairs)]
    psum x1 -> x0, waiting for transfers between devices: 14.2 us -> none  [body(): lax.psum(gate_part.astype(jnp.bfloat16), 'tp').astype(jnp.float32)]
    all_to_all x3 -> x0, starting transfers between devices: 13.6 us -> none  [the longest x1 6.35 us: body(): lax.all_to_all(outgoing, 'blk', split_axis=0, concat_axis=0, tiled=True)]
    dot_general x6 -> x0, matrix products: 12.9 us -> none  [the longest x1 3.41 us: one_block(): jnp.einsum('jzre,ezm->jzrm', weights.astype(jnp.bfloat16), value_block, p...]
    reduce_sum x5 -> x0, other arithmetic: 4.3 us -> none  [the longest x1 3.23 us: one_block(): totals = totals * rescale + jnp.sum(weights, axis=3)]
    ppermute x1 -> x0, starting transfers between devices: 2.77 us -> none  [passed_along(): return lax.ppermute(value, axis, pairs)]
  transfers between devices with their start and end apart: 5 -> 0, of which waited for: 3 -> 0; matrix products, arithmetic and copies ran while one was open for 9% -> 0% of each run, Pallas kernels for 0% -> 0%
where the time goes in v1:
time: 40.4 us; the launch traced here: 40.2 us
  Pallas kernels  35.8 us (89%)
  local copies, waits for them, and re-layouts  3.76 us (9%)
  between operations  0.64 us (2%)
    pallas_call x1, Pallas kernels, body(): pl.pallas_call(functools.partial(kernel, nblk, nside), out_shape=(jax.Sha...  35.8 us
    unnamed x2, local copies, waits for them, and re-layouts  3.76 us

profile of v1, /device:TPU:0, one launch (start us, length us, event | category | flops | bytes accessed | tf_op | source)
XLA Modules:
  0.0 40.2 jit_solution(2691050921363460166)
XLA Ops:
  0.6 35.8 %shard_map.113 = (bf16[128,2048]{1,0:T(8,128)(2,1)}, bf16[128,2048]{1,0:T(8,128)(2,1)}) custom-call(bf16[128,2048]{1,0:T(8,128)(2,1)} %bitcast.18, bf16[128,128]{1,0:T(8,128)(2,1)} %bitcast.22, bf16[128,128]{1,0:T(8,128)(2,1)} %bitcast.23, s32[1,128]{1,0:T(1,128)} %seg_ref.1, bf16[128,2048]{1,0:T(8,128)(2,1)} %bitcast.19, s32[8,128]{1,0:T(8,128)} %bitcast.24, ...), custom_call_target="tpu_custom_call" | custom-call | tf_op jit(solution)/shard_map/pallas_call | solution.py:306
  36.4 1.9 %copy.14 = bf16[1,128,2048]{2,1,0:T(8,128)(2,1)} copy(bf16[1,128,2048]{2,1,0:T(8,128)(2,1)} %bitcast.21) | data formatting | bytes 1048576
  38.3 1.9 %copy.15 = bf16[1,128,2048]{2,1,0:T(8,128)(2,1)} copy(bf16[1,128,2048]{2,1,0:T(8,128)(2,1)} %bitcast.20) | data formatting | bytes 1048576

commit v2 on v1

--- a/solution.py
+++ b/solution.py
@@ -24,12 +24,17 @@
     return jnp.dot(a, b, preferred_element_type=F32)
 
 
+def cuts(width):
+    first = (width // 128 + 1) // 2 * 128
+    return pl.ds(0, first), pl.ds(first, width - first)
+
+
 def kernel(
     nblk, nside,
     q_hbm, k_hbm, v_hbm, seg_ref, x_hbm, ids_ref, rw_ref, wg_hbm, wu_hbm, wd_hbm,
-    att_hbm, moe_hbm,
-    q_ref, kv, segs, x_ref, wg, wu, wd, att, moe,
-    disp, xin, terms, terms_in, zs, zin, hid, po, pin, rs, rin,
+    att_hbm, rin, pull_hbm,
+    q_ref, kv, segs, x_ref, wg, wu, wd, att, pull_ref,
+    disp, xin, terms, terms_in, zs, zin, hid, po, pin, rs,
     in_sem, out_sem,
     kv_ss, kv_rs, sg_ss, sg_rs, d_ss, d_rs, f_ss, f_rs, t_ss, t_rs, z_ss, z_rs,
     h_ss, h_rs, p_ss, p_rs, r_ss, r_rs,
@@ -43,6 +48,8 @@
     quarter = x_ref.shape[1] // 2
     rp = po.shape[1]
     half = nside // 2
+    hidden_cuts = cuts(wg.shape[1])
+    out_cuts = cuts(quarter)
 
     def remote(src, dst, ss, rs_, **where):
         return pltpu.make_async_remote_copy(
@@ -94,13 +101,15 @@
         picks.append(jnp.where(chosen, 1.0, 0.0))
         pulls.append(jnp.where(chosen, shares[e : e + 1, :], 0.0))
     pick = jnp.concatenate(picks, axis=0)
-    pull = jnp.concatenate(pulls, axis=0)
+    pull_ref[...] = jnp.concatenate(pulls, axis=0)
+    pull_out = pltpu.make_async_copy(pull_ref, pull_hbm, out_sem.at[2])
+    pull_out.start()
     segs[b] = seg_ref[...]
     loads[0].wait()
     taken = dot(pick.astype(BF), x_ref[...]).astype(BF)
     for s in range(nblk):
         e, k = s % experts, s // experts
-        disp[s] = taken[e * PAD : (e + 1) * PAD, k * quarter : (k + 1) * quarter]
+        disp[s] = taken[e * PAD : e * PAD + CAP, k * quarter : (k + 1) * quarter]
     xin[j, b] = disp[b]
 
     loads[1].wait()
@@ -154,15 +163,6 @@
             copy.start()
             sends.append(copy)
 
-    m = iota((rp, nblk * PAD), 1)
-    low = m & (PAD - 1)
-    packed = (low < CAP) & ((m >> 4) * CAP + low == iota((rp, nblk * PAD), 0))
-    pack = jnp.where(packed, 1.0, 0.0).astype(BF)
-    r = iota((nblk * PAD, rp), 0)
-    low = r & (PAD - 1)
-    spread = (low < CAP) & ((r >> 4) * CAP + low == iota((nblk * PAD, rp), 1))
-    unpack = jnp.where(spread, 1.0, 0.0).astype(BF)
-
     for d2 in range(1, nside):
         other = at_side(d2)
         for d in range(nblk):
@@ -171,30 +171,31 @@
                 xin.at[other, source], xin.at[other, source], f_ss.at[0, 0],
                 f_rs.at[other, source], side=other,
             ).wait_recv()
-    rows = jnp.concatenate(
-        [
-            dot(pack, xin[s].reshape(nblk * PAD, quarter)).astype(BF)
-            for s in range(nside)
-        ],
-        axis=0,
-    )
-    loads[3].wait()
-    gate = dot(rows, wg[...]).astype(BF)
-    for s in range(nside):
-        terms[s, 0] = gate[s * rp : (s + 1) * rp]
-    loads[4].wait()
-    up = dot(rows, wu[...]).astype(BF)
-    for s in range(nside):
-        terms[s, 1] = up[s * rp : (s + 1) * rp]
-
+    rows = jnp.concatenate([xin[s, i] for s in range(nside) for i in range(nblk)], axis=0)
     mine = pl.ds(t * half, half)
     theirs = pl.ds((1 - t) * half, half)
-    copy = remote(terms.at[theirs], terms_in, t_ss, t_rs, tp=1 - t)
-    copy.start()
-    copy.wait()
-    zs[...] = (terms[mine].astype(F32) + terms_in[...].astype(F32)).astype(BF)
-    z_copy = remote(zs, zin, z_ss, z_rs, blk=at_blk(experts))
-    z_copy.start()
+    loads[3].wait()
+    loads[4].wait()
+    t_copies, z_copies, h_copies = [], [], []
+    for c, cols in enumerate(hidden_cuts):
+        gate = dot(rows, wg[:, cols]).astype(BF)
+        up = dot(rows, wu[:, cols]).astype(BF)
+        for s in range(nside):
+            terms[s, 0, :, cols] = gate[s * rp : (s + 1) * rp]
+            terms[s, 1, :, cols] = up[s * rp : (s + 1) * rp]
+        t_copies.append(remote(
+            terms.at[theirs, :, :, cols], terms_in.at[:, :, :, cols], t_ss.at[c], t_rs.at[c], tp=1 - t
+        ))
+        t_copies[c].start()
+    for c, cols in enumerate(hidden_cuts):
+        t_copies[c].wait()
+        zs[:, :, :, cols] = (
+            terms[mine, :, :, cols].astype(F32) + terms_in[:, :, :, cols].astype(F32)
+        ).astype(BF)
+        z_copies.append(remote(
+            zs.at[:, :, :, cols], zin.at[:, :, :, cols], z_ss.at[c], z_rs.at[c], blk=at_blk(experts)
+        ))
+        z_copies[c].start()
 
     for d in range(1, nblk):
         @pl.when(b - d >= 0)
@@ -232,54 +233,58 @@
     att_out = pltpu.make_async_copy(att, att_hbm, out_sem.at[0])
     att_out.start()
 
-    z_copy.wait()
-    gate_sum = zs[:, 0].astype(F32) + zin[:, 0].astype(F32)
-    up_sum = zs[:, 1].astype(F32) + zin[:, 1].astype(F32)
-    hid[mine] = (jax.nn.silu(gate_sum) * up_sum).astype(BF)
-    copy = remote(hid.at[mine], hid.at[mine], h_ss, h_rs, tp=1 - t)
-    copy.start()
+    for c, cols in enumerate(hidden_cuts):
+        z_copies[c].wait()
+        gate_sum = zs[:, 0, :, cols].astype(F32) + zin[:, 0, :, cols].astype(F32)
+        up_sum = zs[:, 1, :, cols].astype(F32) + zin[:, 1, :, cols].astype(F32)
+        hid[mine, :, cols] = (jax.nn.silu(gate_sum) * up_sum).astype(BF)
+        h_copies.append(remote(
+            hid.at[mine, :, cols], hid.at[mine, :, cols], h_ss.at[c], h_rs.at[c], tp=1 - t
+        ))
+        h_copies[c].start()
     loads[6].wait()
-    copy.wait_send()
-    remote(hid.at[theirs], hid.at[theirs], h_ss, h_rs, tp=1 - t).wait_recv()
-
-    for d in range(1, nside):
-        to = at_side(d)
-        po[to] = dot(hid[to], wd[...]).astype(BF)
-        copy = remote(po.at[to], pin.at[j], p_ss.at[d], p_rs.at[j], side=to)
-        copy.start()
-        sends.append(copy)
-    total = dot(hid[j], wd[...]).astype(BF).astype(F32)
-    for d in range(1, nside):
-        source = at_side(d)
-        remote(po.at[0], pin.at[source], p_ss.at[0], p_rs.at[source], side=source).wait_recv()
-        total = total + pin[source].astype(F32)
-    rs[...] = dot(unpack, total.astype(BF)).astype(BF).reshape(rs.shape)
-    for d in range(1, nblk):
-        to = at_blk(d)
-        copy = remote(rs.at[to], rin.at[b], r_ss.at[d], r_rs.at[b], blk=to)
-        copy.start()
-        sends.append(copy)
-    rin[b] = rs[b]
-
-    width = -(-experts * PAD // 128) * 128
-    if width > experts * PAD:
-        pull = jnp.concatenate([pull, jnp.zeros((width - experts * PAD, length), F32)], axis=0)
-    pull = pull.T[:, : experts * PAD]
-    pull_a = pull.astype(BF)
-    rest = pull - pull_a.astype(F32)
-    pull_b = rest.astype(BF)
-    pull_c = (rest - pull_b.astype(F32)).astype(BF)
-
+    for c, cols in enumerate(hidden_cuts):
+        h_copies[c].wait_send()
+        remote(
+            hid.at[theirs, :, cols], hid.at[theirs, :, cols], h_ss.at[c], h_rs.at[c], tp=1 - t
+        ).wait_recv()
+
+    for c, cols in enumerate(out_cuts):
+        for d in range(1, nside):
+            to = at_side(d)
+            po[to, :, cols] = dot(hid[to], wd[:, cols]).astype(BF)
+            copy = remote(
+                po.at[to, :, cols], pin.at[j, :, cols], p_ss.at[d, c], p_rs.at[j, c], side=to
+            )
+            copy.start()
+            sends.append(copy)
+    totals = [dot(hid[j], wd[:, cols]).astype(BF).astype(F32) for cols in out_cuts]
+    for c, cols in enumerate(out_cuts):
+        total = totals[c]
+        for d in range(1, nside):
+            source = at_side(d)
+            remote(
+                po.at[0, :, cols], pin.at[source, :, cols], p_ss.at[0, c], p_rs.at[source, c], side=source
+            ).wait_recv()
+            total = total + pin[source, :, cols].astype(F32)
+        slot_out = total.astype(BF)
+        for s in range(nblk):
+            rs[s, :, cols] = slot_out[s * CAP : (s + 1) * CAP]
+        for d in order:
+            to = at_blk(d)
+            copy = remote(
+                rs.at[to, :, cols], rin.at[b, :, cols], r_ss.at[d, c], r_rs.at[b, c], blk=to
+            )
+            copy.start()
+            sends.append(copy)
+    own_back = pltpu.make_async_copy(rs.at[b], rin.at[b], out_sem.at[1])
+    own_back.start()
     for d in order:
         source = at_blk(d)
-        remote(rs.at[0], rin.at[source], r_ss.at[0], r_rs.at[source], blk=source).wait_recv()
-    for k in range(2):
-        back = rin[k * experts : (k + 1) * experts].reshape(experts * PAD, quarter)
-        mixed = dot(pull_a, back) + dot(pull_b, back) + dot(pull_c, back)
-        moe[:, k * quarter : (k + 1) * quarter] = mixed.astype(BF)
-    moe_out = pltpu.make_async_copy(moe, moe_hbm, out_sem.at[1])
-    moe_out.start()
-
+        for c, cols in enumerate(out_cuts):
+            remote(
+                rs.at[0, :, cols], rin.at[source, :, cols], r_ss.at[0, c], r_rs.at[source, c], blk=source
+            ).wait_recv()
     for copy in sends:
         copy.wait_send()
     for d in range(1, nblk):
@@ -288,7 +293,47 @@
             for copy in kv_copy(d):
                 copy.wait_send()
     att_out.wait()
-    moe_out.wait()
+    own_back.wait()
+    pull_out.wait()
+
+
+def finish(att_hbm, back_hbm, pull_hbm, out_hbm, moe_hbm, att, back, pull_ref, moe, in_sem, out_sem):
+    loads = [
+        pltpu.make_async_copy(back_hbm, back, in_sem.at[0]),
+        pltpu.make_async_copy(pull_hbm, pull_ref, in_sem.at[1]),
+        pltpu.make_async_copy(att_hbm, att, in_sem.at[2]),
+    ]
+    for load in loads:
+        load.start()
+    nblk, _, quarter = back.shape
+    rows, length = pull_ref.shape
+    loads[1].wait()
+    pull = pull_ref[...]
+    width = -(-rows // 128) * 128
+    if width > rows:
+        pull = jnp.concatenate([pull, jnp.zeros((width - rows, length), F32)], axis=0)
+    pull = pull.T[:, :rows]
+    pull_a = pull.astype(BF)
+    rest = pull - pull_a.astype(F32)
+    pull_b = rest.astype(BF)
+    pull_c = (rest - pull_b.astype(F32)).astype(BF)
+    pull = jnp.concatenate([pull_a, pull_b, pull_c], axis=1)
+    loads[2].wait()
+    stores = [pltpu.make_async_copy(att, out_hbm, out_sem.at[0])]
+    stores[0].start()
+    loads[0].wait()
+    experts = nblk // 2
+    for k in range(2):
+        gap = jnp.zeros((PAD - CAP, quarter), BF)
+        one = jnp.concatenate(
+            [piece for e in range(experts) for piece in (back[k * experts + e], gap)], axis=0
+        )
+        cols = pl.ds(k * quarter, quarter)
+        moe[:, cols] = dot(pull, jnp.concatenate([one] * 3, axis=0)).astype(BF)
+        stores.append(pltpu.make_async_copy(moe.at[:, cols], moe_hbm.at[:, cols], out_sem.at[1 + k]))
+        stores[-1].start()
+    for store in stores:
+        store.wait()
 
 
 def body(
@@ -298,19 +343,21 @@
 ):
     length, width = queries.shape[1:]
     quarter, ff = w_gate.shape[1:]
-    rp = -(-nblk * CAP // PAD) * PAD
+    rp = -(-nblk * CAP // 8) * 8
     half = nside // 2
     vmem = pl.BlockSpec(memory_space=pltpu.VMEM)
     hbm = pl.BlockSpec(memory_space=pl.ANY)
     dma = pltpu.SemaphoreType.DMA
-    attended, moe_out = pl.pallas_call(
+    experts = nblk // 2
+    part_att, back, pull = pl.pallas_call(
         functools.partial(kernel, nblk, nside),
         out_shape=(
             jax.ShapeDtypeStruct((length, width), BF),
-            jax.ShapeDtypeStruct((length, 2 * quarter), BF),
+            jax.ShapeDtypeStruct((nblk, CAP, quarter), BF),
+            jax.ShapeDtypeStruct((experts * PAD, length), F32),
         ),
         in_specs=[hbm, hbm, hbm, vmem, hbm, vmem, vmem, hbm, hbm, hbm],
-        out_specs=(hbm, hbm),
+        out_specs=(hbm, hbm, hbm),
         scratch_shapes=[
             pltpu.VMEM((length, width), BF),
             pltpu.VMEM((nblk, 2, length, HEAD_DIM), BF),
@@ -320,9 +367,9 @@
             pltpu.VMEM((quarter, ff), BF),
             pltpu.VMEM((ff, quarter), BF),
             pltpu.VMEM((length, width), BF),
-            pltpu.VMEM((length, 2 * quarter), BF),
-            pltpu.VMEM((nblk, PAD, quarter), BF),
-            pltpu.VMEM((nside, nblk, PAD, quarter), BF),
+            pltpu.VMEM((experts * PAD, length), F32),
+            pltpu.VMEM((nblk, CAP, quarter), BF),
+            pltpu.VMEM((nside, nblk, CAP, quarter), BF),
             pltpu.VMEM((nside, 2, rp, ff), BF),
             pltpu.VMEM((half, 2, rp, ff), BF),
             pltpu.VMEM((half, 2, rp, ff), BF),
@@ -330,17 +377,16 @@
             pltpu.VMEM((nside, rp, ff), BF),
             pltpu.VMEM((nside, rp, quarter), BF),
             pltpu.VMEM((nside, rp, quarter), BF),
-            pltpu.VMEM((nblk, PAD, quarter), BF),
-            pltpu.VMEM((nblk, PAD, quarter), BF),
+            pltpu.VMEM((nblk, CAP, quarter), BF),
             dma((7,)),
-            dma((2,)),
+            dma((3,)),
             dma((nblk,)), dma((nblk,)),
             dma((nblk,)), dma((nblk,)),
             dma((nblk,)), dma((nblk,)),
             dma((nside, nblk)), dma((nside, nblk)),
-            dma, dma, dma, dma, dma, dma,
-            dma((nside,)), dma((nside,)),
-            dma((nblk,)), dma((nblk,)),
+            dma((2,)), dma((2,)), dma((2,)), dma((2,)), dma((2,)), dma((2,)),
+            dma((nside, 2)), dma((nside, 2)),
+            dma((nblk, 2)), dma((nblk, 2)),
         ],
         compiler_params=pltpu.CompilerParams(
             collective_id=0, has_side_effects=True, vmem_limit_bytes=56 * 1024 * 1024
@@ -350,6 +396,24 @@
         jnp.swapaxes(expert_ids[0], 0, 1), jnp.swapaxes(route_weight[0], 0, 1),
         w_gate[0], w_up[0], w_down[0],
     )
+    attended, moe_out = pl.pallas_call(
+        finish,
+        out_shape=(
+            jax.ShapeDtypeStruct((length, width), BF),
+            jax.ShapeDtypeStruct((length, 2 * quarter), BF),
+        ),
+        in_specs=[hbm, hbm, hbm],
+        out_specs=(hbm, hbm),
+        scratch_shapes=[
+            pltpu.VMEM((length, width), BF),
+            pltpu.VMEM((nblk, CAP, quarter), BF),
+            pltpu.VMEM((experts * PAD, length), F32),
+            pltpu.VMEM((length, 2 * quarter), BF),
+            dma((3,)),
+            dma((3,)),
+        ],
+        compiler_params=pltpu.CompilerParams(vmem_limit_bytes=60 * 1024 * 1024),
+    )(part_att, back, pull)
     return attended[None], moe_out[None]
 
 

time: 40.4 us -> 35 us (0.87)
  local copies, waits for them, and re-layouts: 3.76 us -> 0 us
  Pallas kernels: 35.8 us -> 34.1 us
    pallas_call x1, Pallas kernels: 35.8 us -> 31.9 us  [body(): pl.pallas_call(functools.partial(kernel, nblk, nside), out_shape=(jax.Sha...]
    unnamed x2 -> x0, local copies, waits for them, and re-layouts: 3.76 us -> none
    pallas_call x0 -> x1, Pallas kernels: none -> 2.19 us  [body(): pl.pallas_call(finish, out_shape=(jax.ShapeDtypeStruct((length, width), B...]
where the time goes in v2:
time: 35 us; the launch traced here: 34.8 us
  Pallas kernels  34.1 us (97%)
  between operations  0.64 us (2%)
    pallas_call x1, Pallas kernels, body(): pl.pallas_call(functools.partial(kernel, nblk, nside), out_shape=(jax.Sha...  31.9 us
    pallas_call x1, Pallas kernels, body(): pl.pallas_call(finish, out_shape=(jax.ShapeDtypeStruct((length, width), B...  2.19 us

profile of v2, /device:TPU:0, one launch (start us, length us, event | category | flops | bytes accessed | tf_op | source)
XLA Modules:
  0.0 34.8 jit_solution(12187677182937732458)
XLA Ops:
  0.6 31.9 %shard_map.113 = (bf16[128,2048]{1,0:T(8,128)(2,1)}, bf16[4,10,1024]{2,1,0:T(8,128)(2,1)}, f32[32,128]{1,0:T(8,128)}) custom-call(bf16[128,2048]{1,0:T(8,128)(2,1)} %bitcast.18, bf16[128,128]{1,0:T(8,128)(2,1)} %bitcast.20, bf16[128,128]{1,0:T(8,128)(2,1)} %bitcast.21, s32[1,128]{1,0:T(1,128)} %seg_ref.1, bf16[128,2048]{1,0:T(8,128)(2,1)} %bitcast.19, ...), custom_call_target="tpu_custom_call" | custom-call | tf_op jit(solution)/shard_map/pallas_call | solution.py:352
  32.6 2.2 %shard_map.114 = (bf16[128,2048]{1,0:T(8,128)(2,1)}, bf16[128,2048]{1,0:T(8,128)(2,1)}) custom-call(bf16[128,2048]{1,0:T(8,128)(2,1)} %get-tuple-element.7.att_hbm, bf16[4,10,1024]{2,1,0:T(8,128)(2,1)} %get-tuple-element.8.back_hbm, f32[32,128]{1,0:T(8,128)} %get-tuple-element.9.pull_hbm), custom_call_target="tpu_custom_call" | custom-call | tf_op jit(solution)/shard_map/pallas_call | solution.py:399
